TPU v7x, 512 devices: a whole 4x4x16 slice. The times are simulated.
512 devices in a mesh: cb: 16 (over z_lo, core), frame: 32 (over x, y, z_hi).
Axes of the slice: x: 4, y: 4, z: 16 (z_hi: 2, z_lo: 8; z = z_hi * 8 + z_lo), core: 2. Of those that a mesh axis runs over, the one named last changes fastest.
Arguments:
- inputs: bfloat16 [8192, 16, 1024], P('frame', 'cb'), may hold values from -64 to 64
- norm_gain: float32 [1024], replicated, may hold values from 0.1 to 1.9
- w_qkv: bfloat16 [16, 1024, 3072], P('cb', 'frame'), may hold values from -4 to 4
- w_out: bfloat16 [16, 1024, 1024], P('cb', 'frame'), may hold values from -0.1875 to 0.1875
- grad_out: bfloat16 [8192, 16, 1024], P('frame', 'cb'), may hold values from -6 to 6
Outputs:
- outputs: bfloat16 [8192, 16, 1024], P('frame', 'cb')
- grad_in: bfloat16 [8192, 16, 1024], P('frame', 'cb')
All inputs are finite; a program needn't handle non-finite values.
Results may differ from a plain program's by a relative error of at most 0.0053.
Values may be sent and summed in bfloat16 or wider, within the bound.
A program may use at most 64 MiB of HBM per device.

v0:
```python
import jax
import jax.numpy as jnp
from jax import lax
from jax.sharding import PartitionSpec as P

HEADS = 16


epsilon = 1e-05


def to_heads(values, head_count):
    frames, depth, columns = values.shape
    return values.reshape(frames, depth, head_count, columns // head_count)


def attention_probs(queries, key_rows, head_count):
    depth = queries.shape[1]
    factor = (queries.shape[2] // head_count) ** (-0.5)
    scores = (
        jnp.einsum(
            "fihe,fjhe->fhij",
            to_heads(queries, head_count),
            to_heads(key_rows, head_count),
            preferred_element_type=jnp.float32,
        )
        * factor
    )
    causal = lax.broadcasted_iota(jnp.int32, (depth, depth), 0) >= lax.broadcasted_iota(
        jnp.int32, (depth, depth), 1
    )
    scores = jnp.where(causal, scores, -jnp.inf)
    weights = jnp.exp(scores - jnp.max(scores, axis=-1, keepdims=True))
    return weights / jnp.sum(weights, axis=-1, keepdims=True)


def attend_all(queries, key_rows, values, head_count):
    probs_low = attention_probs(queries, key_rows, head_count).astype(jnp.bfloat16)
    mixed = jnp.einsum(
        "fhij,fjhe->fihe",
        probs_low,
        to_heads(values, head_count),
        preferred_element_type=jnp.float32,
    )
    return mixed.reshape(values.shape).astype(jnp.bfloat16)


def attention_grads(queries, key_rows, values, grad_context, head_count):
    shape_full = queries.shape
    factor = (queries.shape[2] // head_count) ** (-0.5)
    probs = attention_probs(queries, key_rows, head_count)
    probs_low = probs.astype(jnp.bfloat16)
    grad_heads = to_heads(grad_context, head_count)
    grad_values = jnp.einsum(
        "fhij,fihe->fjhe", probs_low, grad_heads, preferred_element_type=jnp.float32
    )
    grad_probs = jnp.einsum(
        "fihe,fjhe->fhij",
        grad_heads,
        to_heads(values, head_count),
        preferred_element_type=jnp.float32,
    )
    inner = jnp.sum(probs * grad_probs, axis=-1, keepdims=True)
    grad_scores = (probs * (grad_probs - inner) * factor).astype(jnp.bfloat16)
    grad_queries = jnp.einsum(
        "fhij,fjhe->fihe",
        grad_scores,
        to_heads(key_rows, head_count),
        preferred_element_type=jnp.float32,
    )
    grad_keys = jnp.einsum(
        "fhij,fihe->fjhe",
        grad_scores,
        to_heads(queries, head_count),
        preferred_element_type=jnp.float32,
    )
    return (
        grad_queries.reshape(shape_full).astype(jnp.bfloat16),
        grad_keys.reshape(shape_full).astype(jnp.bfloat16),
        grad_values.reshape(shape_full).astype(jnp.bfloat16),
    )


def body(inputs, norm_gain, w_qkv, w_out, grad_out):
    frames, local_cb, columns = inputs.shape
    wide_in = inputs.astype(jnp.float32)
    inverse_rms = lax.rsqrt(jnp.mean(wide_in * wide_in, axis=-1, keepdims=True) + epsilon)
    normed = (wide_in * inverse_rms * norm_gain).astype(jnp.bfloat16)
    full_qkv, full_out = (
        lax.all_gather(w_qkv, "frame", axis=1, tiled=True),
        lax.all_gather(w_out, "frame", axis=1, tiled=True),
    )
    projected = jnp.einsum(
        "fcd,cde->fce", normed, full_qkv, preferred_element_type=jnp.float32
    ).astype(jnp.bfloat16)
    queries = projected[:, :, :columns]
    key_rows = projected[:, :, columns : 2 * columns]
    values = projected[:, :, 2 * columns :]
    grad_context = jnp.einsum(
        "fce,cde->fcd", grad_out, full_out, preferred_element_type=jnp.float32
    ).astype(jnp.bfloat16)
    own_q, own_k, own_v = (
        lax.all_to_all(queries, "cb", split_axis=0, concat_axis=1, tiled=True),
        lax.all_to_all(key_rows, "cb", split_axis=0, concat_axis=1, tiled=True),
        lax.all_to_all(values, "cb", split_axis=0, concat_axis=1, tiled=True),
    )
    own_context = attend_all(own_q, own_k, own_v, HEADS)
    context = lax.all_to_all(own_context, "cb", split_axis=1, concat_axis=0, tiled=True)
    own_grad = lax.all_to_all(grad_context, "cb", split_axis=0, concat_axis=1, tiled=True)
    grad_q, grad_k, grad_v = attention_grads(own_q, own_k, own_v, own_grad, HEADS)
    back_q, back_k, back_v = (
        lax.all_to_all(grad_q, "cb", split_axis=1, concat_axis=0, tiled=True),
        lax.all_to_all(grad_k, "cb", split_axis=1, concat_axis=0, tiled=True),
        lax.all_to_all(grad_v, "cb", split_axis=1, concat_axis=0, tiled=True),
    )
    outputs = (
        wide_in + jnp.einsum("fcd,cde->fce", context, full_out, preferred_element_type=jnp.float32)
    ).astype(jnp.bfloat16)
    grad_qkv = jnp.concatenate([back_q, back_k, back_v], axis=-1)
    scaled = (
        jnp.einsum("fce,cde->fcd", grad_qkv, full_qkv, preferred_element_type=jnp.float32)
        * norm_gain
    )
    inner = jnp.mean(scaled * wide_in, axis=-1, keepdims=True)
    grad_in = grad_out.astype(jnp.float32) + inverse_rms * (
        scaled - wide_in * inverse_rms * inverse_rms * inner
    )
    return (outputs, grad_in.astype(jnp.bfloat16))


def solution(mesh):
    return jax.shard_map(
        body,
        mesh=mesh,
        in_specs=(
            P("frame", "cb", None),
            P(),
            P("cb", "frame", None),
            P("cb", "frame", None),
            P("frame", "cb", None),
        ),
        out_specs=(P("frame", "cb", None), P("frame", "cb", None)),
        check_vma=False,
    )
```

profile of v0, /device:TPU:1, one launch (start us, length us, event | category | flops | bytes accessed | tf_op | source)
XLA Modules:
  0.0 611.5 jit_solution(16031398221519742977)
XLA Ops:
  8.6 139.1 %all-gather.5.cloned.1.call-done = bf16[1,1024,1024]{2,1,0:T(8,128)(2,1)} async-done(((bf16[1,32,1024]{2,1,0:T(8,128)(2,1)}), bf16[1,1024,1024]{2,1,0:T(8,128)(2,1)}) %all-gather.5.cloned.1.call-update) | async-done | bytes 2097168 | tf_op jit(solution)/shard_map/all_gather | solution.py:91
  147.7 2.4 fusion.54
  153.0 5.7 all-to-all-start.4
  158.9 204.3 %all-gather.3.cloned.1.call-done = bf16[1,1024,3072]{2,1,0:T(8,128)(2,1)} async-done(((bf16[1,32,3072]{2,1,0:T(8,128)(2,1)}), bf16[1,1024,3072]{2,1,0:T(8,128)(2,1)}) %all-gather.3.cloned.1.call-update) | async-done | bytes 6291472 | tf_op jit(solution)/shard_map/all_gather | solution.py:90
  363.3 4.6 fusion.9
  370.2 5.2 all-to-all-start.2
  377.5 24.1 %all-to-all-done.2 = bf16[16,2,8192]{2,1,0:T(2,128)(2,1)S(1)} async-done(((bf16[16,2,8192]{2,1,0:T(2,128)(2,1)}), bf16[16,2,8192]{2,1,0:T(2,128)(2,1)S(1)}, u32[]{:S(2)}, u32[]{:S(2)}) %all-to-all-start.2) | async-done | bytes 524320 | tf_op jit(solution)/shard_map/all_to_all | solution.py:104
  401.7 7.0 %all-to-all-start.1 = ((bf16[16,2,8192]{2,1,0:T(2,128)(2,1)}), bf16[16,2,8192]{2,1,0:T(2,128)(2,1)S(1)}, u32[]{:S(2)}, u32[]{:S(2)}) async-start(bf16[16,2,8192]{2,1,0:T(2,128)(2,1)} %reshape.110), calls=%async_computation.1 | async-start | bytes 1048576 | tf_op jit(solution)/shard_map/all_to_all | solution.py:103
  410.8 24.1 %all-to-all-done.1 = bf16[16,2,8192]{2,1,0:T(2,128)(2,1)S(1)} async-done(((bf16[16,2,8192]{2,1,0:T(2,128)(2,1)}), bf16[16,2,8192]{2,1,0:T(2,128)(2,1)S(1)}, u32[]{:S(2)}, u32[]{:S(2)}) %all-to-all-start.1) | async-done | bytes 524320 | tf_op jit(solution)/shard_map/all_to_all | solution.py:103
  434.9 7.1 %all-to-all-start = ((bf16[16,2,8192]{2,1,0:T(2,128)(2,1)}), bf16[16,2,8192]{2,1,0:T(2,128)(2,1)S(1)}, u32[]{:S(2)}, u32[]{:S(2)}) async-start(bf16[16,2,8192]{2,1,0:T(2,128)(2,1)} %reshape.106), calls=%async_computation | async-start | bytes 1048576 | tf_op jit(solution)/shard_map/all_to_all | solution.py:105
  443.3 2.2 reshape.109
  445.7 1.7 reshape.104
  447.4 2.2 reshape.111
  450.5 4.9 fusion.95
  455.4 2.5 fusion.30
  459.7 8.5 %all-to-all-done = bf16[16,2,8192]{2,1,0:T(2,128)(2,1)S(1)} async-done(((bf16[16,2,8192]{2,1,0:T(2,128)(2,1)}), bf16[16,2,8192]{2,1,0:T(2,128)(2,1)S(1)}, u32[]{:S(2)}, u32[]{:S(2)}) %all-to-all-start) | async-done | bytes 524320 | tf_op jit(solution)/shard_map/all_to_all | solution.py:105
  468.2 7.1 %all-to-all-start.7 = ((bf16[16,16,1024]{2,0,1:T(8,128)(2,1)}), bf16[16,16,1024]{2,0,1:T(8,128)(2,1)}, u32[]{:S(2)}, u32[]{:S(2)}) async-start(bf16[16,16,1024]{2,0,1:T(8,128)(2,1)} %reshape.101), calls=%async_computation.7 | async-start | bytes 1048576 | tf_op jit(solution)/shard_map/all_to_all | solution.py:114
  476.6 2.6 fusion.71
  479.2 5.8 fusion.29
  485.0 1.6 copy.88
  488.1 13.5 %all-to-all-done.7 = bf16[16,16,1024]{2,0,1:T(8,128)(2,1)} async-done(((bf16[16,16,1024]{2,0,1:T(8,128)(2,1)}), bf16[16,16,1024]{2,0,1:T(8,128)(2,1)}, u32[]{:S(2)}, u32[]{:S(2)}) %all-to-all-start.7) | async-done | bytes 524320 | tf_op jit(solution)/shard_map/all_to_all | solution.py:114
  501.6 7.1 %all-to-all-start.6 = ((bf16[16,16,1024]{2,0,1:T(8,128)(2,1)}), bf16[16,16,1024]{2,0,1:T(8,128)(2,1)}, u32[]{:S(2)}, u32[]{:S(2)}) async-start(bf16[16,16,1024]{2,0,1:T(8,128)(2,1)} %reshape.100), calls=%async_computation.6 | async-start | bytes 1048576 | tf_op jit(solution)/shard_map/all_to_all | solution.py:113
  508.6 5.9 fusion.28
  517.6 17.4 %all-to-all-done.6 = bf16[16,16,1024]{2,0,1:T(8,128)(2,1)} async-done(((bf16[16,16,1024]{2,0,1:T(8,128)(2,1)}), bf16[16,16,1024]{2,0,1:T(8,128)(2,1)}, u32[]{:S(2)}, u32[]{:S(2)}) %all-to-all-start.6) | async-done | bytes 524320 | tf_op jit(solution)/shard_map/all_to_all | solution.py:113
  535.0 7.1 %all-to-all-start.5 = ((bf16[16,16,1024]{2,0,1:T(8,128)(2,1)}), bf16[16,16,1024]{2,0,1:T(8,128)(2,1)S(1)}, u32[]{:S(2)}, u32[]{:S(2)}) async-start(bf16[16,16,1024]{2,0,1:T(8,128)(2,1)} %reshape.99), calls=%async_computation.5 | async-start | bytes 1048576 | tf_op jit(solution)/shard_map/all_to_all | solution.py:112
  542.0 2.5 fusion.27
  544.8 1.5 reshape.98
  546.3 21.9 %all-to-all-done.5 = bf16[16,16,1024]{2,0,1:T(8,128)(2,1)S(1)} async-done(((bf16[16,16,1024]{2,0,1:T(8,128)(2,1)}), bf16[16,16,1024]{2,0,1:T(8,128)(2,1)S(1)}, u32[]{:S(2)}, u32[]{:S(2)}) %all-to-all-start.5) | async-done | bytes 524320 | tf_op jit(solution)/shard_map/all_to_all | solution.py:112
  568.3 7.1 %all-to-all-start.3 = ((bf16[16,16,1024]{2,0,1:T(8,128)(2,1)}), bf16[16,16,1024]{2,0,1:T(8,128)(2,1)S(1)}, u32[]{:S(2)}, u32[]{:S(2)}) async-start(bf16[16,16,1024]{2,0,1:T(8,128)(2,1)} %reshape.98), calls=%async_computation.3 | async-start | bytes 1048576 | tf_op jit(solution)/shard_map/all_to_all | solution.py:108
  575.3 5.1 fusion.64
  581.6 19.9 %all-to-all-done.3 = bf16[16,16,1024]{2,0,1:T(8,128)(2,1)S(1)} async-done(((bf16[16,16,1024]{2,0,1:T(8,128)(2,1)}), bf16[16,16,1024]{2,0,1:T(8,128)(2,1)S(1)}, u32[]{:S(2)}, u32[]{:S(2)}) %all-to-all-start.3) | async-done | bytes 524320 | tf_op jit(solution)/shard_map/all_to_all | solution.py:108
  601.5 3.1 fusion.42
  (54 shorter events, 22.5 us)
Async XLA Ops:
  7.2 140.6 %all-gather.5.cloned.1.call-start = ((), (), s32[]{:S(2)}) async-start(), calls=%async_computation.9 | async-start | bytes 2162688 | tf_op jit(solution)/shard_map/all_gather | solution.py:91
  7.9 355.4 %all-gather.3.cloned.1.call-start = ((), (), s32[]{:S(2)}) async-start(), calls=%async_computation.8 | async-start | bytes 6488064 | tf_op jit(solution)/shard_map/all_gather | solution.py:90
  150.6 8.1 %copy-start.2 = (bf16[256,1,1024]{2,0,1:T(8,128)(2,1)S(1)}, bf16[256,1,1024]{2,0,1:T(8,128)(2,1)}, u32[]{:S(2)}) copy-start(bf16[256,1,1024]{2,0,1:T(8,128)(2,1)} %param.5) | copy-start | bytes 1572868
  151.6 211.6 %copy-start.8 = (f32[1024]{0:T(1024)S(1)}, f32[1024]{0:T(1024)}, u32[]{:S(2)}) copy-start(f32[1024]{0:T(1024)} %param.6) | copy-start | bytes 12292
  153.0 217.1 %all-to-all-start.4 = ((bf16[16,2,8192]{2,1,0:T(2,128)(2,1)}), bf16[16,2,8192]{2,1,0:T(2,128)(2,1)S(1)}, u32[]{:S(2)}, u32[]{:S(2)}) async-start(bf16[16,2,8192]{2,1,0:T(2,128)(2,1)} %reshape.112), calls=%async_computation.4 | async-start | bytes 1048576 | tf_op jit(solution)/shard_map/all_to_all | solution.py:109
  370.2 31.5 %all-to-all-start.2 = ((bf16[16,2,8192]{2,1,0:T(2,128)(2,1)}), bf16[16,2,8192]{2,1,0:T(2,128)(2,1)S(1)}, u32[]{:S(2)}, u32[]{:S(2)}) async-start(bf16[16,2,8192]{2,1,0:T(2,128)(2,1)} %reshape.108), calls=%async_computation.2 | async-start | bytes 1048576 | tf_op jit(solution)/shard_map/all_to_all | solution.py:104
  401.7 40.3 %copy-start = (bf16[16,2,8192]{2,1,0:T(2,128)(2,1)}, bf16[16,2,8192]{2,1,0:T(2,128)(2,1)S(1)}, u32[]{:S(2)}) copy-start(bf16[16,2,8192]{2,1,0:T(2,128)(2,1)S(1)} %all-to-all-done.2) | copy-start | bytes 1572868
  401.7 33.2 %all-to-all-start.1 = ((bf16[16,2,8192]{2,1,0:T(2,128)(2,1)}), bf16[16,2,8192]{2,1,0:T(2,128)(2,1)S(1)}, u32[]{:S(2)}, u32[]{:S(2)}) async-start(bf16[16,2,8192]{2,1,0:T(2,128)(2,1)} %reshape.110), calls=%async_computation.1 | async-start | bytes 1048576 | tf_op jit(solution)/shard_map/all_to_all | solution.py:103
  434.9 7.1 %copy-start.1 = (bf16[16,2,8192]{2,1,0:T(2,128)(2,1)}, bf16[16,2,8192]{2,1,0:T(2,128)(2,1)S(1)}, u32[]{:S(2)}) copy-start(bf16[16,2,8192]{2,1,0:T(2,128)(2,1)S(1)} %all-to-all-done.1) | copy-start | bytes 1572868
  434.9 33.3 %all-to-all-start = ((bf16[16,2,8192]{2,1,0:T(2,128)(2,1)}), bf16[16,2,8192]{2,1,0:T(2,128)(2,1)S(1)}, u32[]{:S(2)}, u32[]{:S(2)}) async-start(bf16[16,2,8192]{2,1,0:T(2,128)(2,1)} %reshape.106), calls=%async_computation | async-start | bytes 1048576 | tf_op jit(solution)/shard_map/all_to_all | solution.py:105
  450.5 4.9 copy-start.5
  468.2 33.4 %all-to-all-start.7 = ((bf16[16,16,1024]{2,0,1:T(8,128)(2,1)}), bf16[16,16,1024]{2,0,1:T(8,128)(2,1)}, u32[]{:S(2)}, u32[]{:S(2)}) async-start(bf16[16,16,1024]{2,0,1:T(8,128)(2,1)} %reshape.101), calls=%async_computation.7 | async-start | bytes 1048576 | tf_op jit(solution)/shard_map/all_to_all | solution.py:114
  476.6 2.6 copy-start.6
  485.0 23.6 %copy-start.4 = (bf16[16,16,16,64]{3,2,0,1:T(8,128)(2,1)S(1)}, bf16[16,16,16,64]{3,2,0,1:T(8,128)(2,1)}, u32[]{:S(2)}) copy-start(bf16[16,16,16,64]{3,2,0,1:T(8,128)(2,1)} %reshape.104) | copy-start | bytes 1572868
  501.6 33.4 %all-to-all-start.6 = ((bf16[16,16,1024]{2,0,1:T(8,128)(2,1)}), bf16[16,16,1024]{2,0,1:T(8,128)(2,1)}, u32[]{:S(2)}, u32[]{:S(2)}) async-start(bf16[16,16,1024]{2,0,1:T(8,128)(2,1)} %reshape.100), calls=%async_computation.6 | async-start | bytes 1048576 | tf_op jit(solution)/shard_map/all_to_all | solution.py:113
  535.0 33.3 %all-to-all-start.5 = ((bf16[16,16,1024]{2,0,1:T(8,128)(2,1)}), bf16[16,16,1024]{2,0,1:T(8,128)(2,1)S(1)}, u32[]{:S(2)}, u32[]{:S(2)}) async-start(bf16[16,16,1024]{2,0,1:T(8,128)(2,1)} %reshape.99), calls=%async_computation.5 | async-start | bytes 1048576 | tf_op jit(solution)/shard_map/all_to_all | solution.py:112
  544.5 30.8 %copy-start.3 = (bf16[256,1,1024]{2,0,1:T(8,128)(2,1)S(1)}, bf16[256,1,1024]{2,0,1:T(8,128)(2,1)}, u32[]{:S(2)}) copy-start(bf16[256,1,1024]{2,0,1:T(8,128)(2,1)} %param.5) | copy-start | bytes 1572868
  568.3 33.3 %all-to-all-start.3 = ((bf16[16,16,1024]{2,0,1:T(8,128)(2,1)}), bf16[16,16,1024]{2,0,1:T(8,128)(2,1)S(1)}, u32[]{:S(2)}, u32[]{:S(2)}) async-start(bf16[16,16,1024]{2,0,1:T(8,128)(2,1)} %reshape.98), calls=%async_computation.3 | async-start | bytes 1048576 | tf_op jit(solution)/shard_map/all_to_all | solution.py:108
  575.3 5.1 copy-start.7
Sparse Core Ops, SparseCore 0:
  12.3 135.4 all-gather.4
  152.0 211.2 all-gather.2
where the time goes:
time: 613 us; the launch traced here: 611 us
  waiting for transfers between devices  474 us (77%)
  starting transfers between devices  53.3 us (9%)
  matrix products  39.4 us (6%)
  local copies, waits for them, and re-layouts  25.1 us (4%)
  between operations  14.3 us (2%)
    all_gather x1, waiting for transfers between devices, body(): lax.all_gather(w_qkv, 'frame', axis=1, tiled=True)  204 us
    all_gather x1, waiting for transfers between devices, body(): lax.all_gather(w_out, 'frame', axis=1, tiled=True)  139 us
    all_to_all x1, waiting for transfers between devices, body(): lax.all_to_all(key_rows, 'cb', split_axis=0, concat_axis=1, tiled=True)  24.1 us
    all_to_all x1, waiting for transfers between devices, body(): lax.all_to_all(queries, 'cb', split_axis=0, concat_axis=1, tiled=True)  24.1 us
    all_to_all x1, waiting for transfers between devices, body(): lax.all_to_all(grad_q, 'cb', split_axis=1, concat_axis=0, tiled=True)  21.9 us
    all_to_all x1, waiting for transfers between devices, body(): lax.all_to_all(own_context, 'cb', split_axis=1, concat_axis=0, tiled=True)  19.9 us
    all_to_all x1, waiting for transfers between devices, body(): lax.all_to_all(grad_k, 'cb', split_axis=1, concat_axis=0, tiled=True)  17.4 us
    all_to_all x1, waiting for transfers between devices, body(): lax.all_to_all(grad_v, 'cb', split_axis=1, concat_axis=0, tiled=True)  13.5 us
  transfers between devices with their start and end apart: 10, of which 9 were waited for; matrix products, arithmetic and copies ran while one was open for 11% of the time, Pallas kernels for 0%

commit v1 on v0

v1 whole, which is shorter than its diff:
```python
import jax
import jax.numpy as jnp
from jax import lax
from jax.experimental import pallas as pl
from jax.experimental.pallas import tpu as pltpu
from jax.sharding import PartitionSpec as P

D = 1024
CB = 16
FR = 256
FG = FR // CB
HALF = D // 2
EPS = 1e-05
BF = jnp.bfloat16
F32 = jnp.float32
NT = (((1,), (1,)), ((), ()))
NN = (((1,), (0,)), ((), ()))
TN = (((0,), (0,)), ((), ()))


def dot(a, b, dims):
    return lax.dot_general(a, b, dims, preferred_element_type=F32)


def kernel(
    x_ref, gain_ref, wqkv_ref, wout_ref, g_ref, out_ref, gin_ref,
    w, normed, fwd, got, back, home, gn,
    gsend, grecv, lsem, fsend, frecv, bsend, brecv,
):
    cb = lax.axis_index("cb")
    fr = lax.axis_index("frame")
    x, y, zh = fr // 8, (fr // 2) % 4, fr % 2
    xr, xl = (x + 1) % 4, (x + 3) % 4
    yr, yl = (y + 1) % 4, (y + 3) % 4

    def at(xx, yy, zz):
        return {"frame": (xx * 4 + yy) * 2 + zz}

    barrier = pltpu.get_barrier_semaphore()
    for peer in (at(x, y, 1 - zh), at(xr, y, zh), at(xl, y, zh), at(x, yr, zh), at(x, yl, zh)):
        pl.semaphore_signal(barrier, inc=1, device_id=peer)

    @pl.loop(1, CB)
    def _(j):
        pl.semaphore_signal(barrier, inc=1, device_id={"cb": (cb + j) % CB})

    pl.semaphore_wait(barrier, 5 + CB - 1)

    def shard(p):
        if p == 0:
            return wout_ref
        return wqkv_ref.at[:, pl.ds((3 - p) * D, D)]

    def remote(src, dst, p, s, peer):
        return pltpu.make_async_remote_copy(
            src_ref=src, dst_ref=dst, send_sem=gsend.at[p, s], recv_sem=grecv.at[p, s],
            device_id=peer, device_id_type=pl.DeviceIdType.MESH,
        )

    cols = (pl.ds(0, HALF), pl.ds(HALF, HALF))
    copies = {}

    def start(key, copy):
        copy.start()
        copies[key] = copy

    def begin(p):
        own = w.at[p, x, y, pl.ds(zh * 32, 32), :]
        start((p, 0), remote(shard(p), own, p, 0, at(x, y, 1 - zh)))
        local = pltpu.make_async_copy(shard(p), own, lsem.at[p])
        local.start()
        copies[p] = local

    def tick0(p):
        copies[p].wait()
        copies[p, 0].wait_recv()
        for h, right, left in ((0, at(xr, y, zh), at(xl, y, zh)), (1, at(x, yr, zh), at(x, yl, zh))):
            block = w.at[p, x, y, :, cols[h]]
            start((p, 1 + 4 * h), remote(block, block, p, 1 + 4 * h, right))
            start((p, 2 + 4 * h), remote(block, block, p, 2 + 4 * h, left))

    def tick1(p):
        for h, right, left in ((0, at(xr, y, zh), at(xl, y, zh)), (1, at(x, yr, zh), at(x, yl, zh))):
            copies[p, 1 + 4 * h].wait_recv()
            fx, fy = ((xl, y), (x, yl))[h]
            block = w.at[p, fx, fy, pl.ds(0, 32), cols[h]]
            start((p, 3 + 4 * h), remote(block, block, p, 3 + 4 * h, right))
        for h, right, left in ((0, at(xr, y, zh), at(xl, y, zh)), (1, at(x, yr, zh), at(x, yl, zh))):
            copies[p, 2 + 4 * h].wait_recv()
            fx, fy = ((xr, y), (x, yr))[h]
            block = w.at[p, fx, fy, pl.ds(32, 32), cols[h]]
            start((p, 4 + 4 * h), remote(block, block, p, 4 + 4 * h, left))

    def line(p, h, pos, part):
        span = (slice(None), pl.ds(0, 2), pl.ds(2, 2))[part]
        if h == 0:
            return w.at[p, span, pos, :, cols[0]]
        return w.at[p, pos, span, :, cols[1]]

    def tick2(p):
        for h in range(2):
            copies[p, 3 + 4 * h].wait_recv()
            copies[p, 4 + 4 * h].wait_recv()
            right, left = ((at(x, yr, zh), at(x, yl, zh)), (at(xr, y, zh), at(xl, y, zh)))[h]
            block = line(p, h, (y, x)[h], 0)
            start((p, 9 + 4 * h), remote(block, block, p, 9 + 4 * h, right))
            start((p, 10 + 4 * h), remote(block, block, p, 10 + 4 * h, left))

    def tick3(p):
        for h in range(2):
            right, left = ((at(x, yr, zh), at(x, yl, zh)), (at(xr, y, zh), at(xl, y, zh)))[h]
            copies[p, 9 + 4 * h].wait_recv()
            block = line(p, h, (yl, xl)[h], 1)
            start((p, 11 + 4 * h), remote(block, block, p, 11 + 4 * h, right))
            copies[p, 10 + 4 * h].wait_recv()
            block = line(p, h, (yr, xr)[h], 2)
            start((p, 12 + 4 * h), remote(block, block, p, 12 + 4 * h, left))

    def tick4(p):
        for s in (11, 12, 15, 16):
            copies[p, s].wait_recv()

    def exchange(src, dst, ssem, rsem, t, c):
        part = cols[c]

        @pl.loop(0, CB)
        def _(j):
            peer = (cb + 8 + j) % CB

            @pl.when(j != 8)
            def _():
                pltpu.make_async_remote_copy(
                    src_ref=src.at[t, peer, :, part], dst_ref=dst.at[t, cb, :, part],
                    send_sem=ssem.at[t, c], recv_sem=rsem.at[t, c],
                    device_id={"cb": peer}, device_id_type=pl.DeviceIdType.MESH,
                ).start()

        pltpu.make_async_copy(
            src.at[t, cb, :, part], dst.at[t, cb, :, part], rsem.at[t, c]
        ).start()

    def arrived(dst, rsem, t, c):
        whole = dst.at[t, :, :, cols[c]]
        pltpu.make_async_copy(whole, whole, rsem.at[t, c]).wait()

    def sent(src, ssem, t, c):
        most = src.at[t, pl.ds(0, CB - 1), :, cols[c]]
        pltpu.make_async_copy(most, most, ssem.at[t, c]).wait()

    def project(p):
        for c in range(2):

            @pl.loop(0, 2)
            def _(i):
                col = pl.multiple_of((2 * c + i) * 256, 256)
                if p == 0:
                    tile = dot(g_ref[...], w[0, 2 * c + i].reshape(256, D), NT)
                else:
                    tile = dot(normed[...], w[p, :, :, :, pl.ds(col, 256)].reshape(D, 256), NN)
                fwd[p, :, :, pl.ds(col, 256)] = tile.astype(BF).reshape(CB, FG, 256)

            exchange(fwd, got, fsend, frecv, p, c)

    for p in range(4):
        begin(p)

    @pl.loop(0, 8)
    def _(i):
        rows = pl.ds(pl.multiple_of(i * 32, 32), 32)
        wide = x_ref[rows, :].astype(F32)
        r = lax.rsqrt(jnp.mean(wide * wide, axis=-1, keepdims=True) + EPS)
        normed[rows, :] = (wide * r * gain_ref[...]).astype(BF)

    tick0(0), tick1(0), tick2(0), tick0(1)
    tick3(0), tick1(1), tick4(0)
    project(0)
    tick2(1), tick0(2)
    tick3(1), tick1(2), tick4(1)
    project(1)
    tick2(2), tick0(3)
    tick3(2), tick1(3), tick4(2)
    project(2)
    tick2(3), tick3(3), tick4(3)
    project(3)

    ri = lax.broadcasted_iota(jnp.int32, (FR, FR), 0)
    ci = lax.broadcasted_iota(jnp.int32, (FR, FR), 1)
    seen = jnp.logical_and((ri & (FG - 1)) == (ci & (FG - 1)), ri >= ci)
    low = lax.broadcasted_iota(jnp.int32, (FR, 128), 1) < 64
    zero = jnp.zeros((FR, 128), BF)

    for c in range(2):
        for t in range(4):
            arrived(got, frecv, t, c)

        @pl.loop(0, 4)
        def _(i):
            part = pl.ds(pl.multiple_of(c * HALF + i * 128, 128), 128)
            gc, v, k, q = (got[t, :, :, part].reshape(FR, 128) for t in range(4))
            results = []
            for mine in (low, jnp.logical_not(low)):
                scores = jnp.where(seen, dot(jnp.where(mine, q, zero), k, NT) * 0.125, -jnp.inf)
                e = jnp.exp(scores - jnp.max(scores, axis=-1, keepdims=True))
                probs = e / jnp.sum(e, axis=-1, keepdims=True)
                rough = probs.astype(BF)
                gp = dot(jnp.where(mine, gc, zero), v, NT)
                inner = jnp.sum(probs * gp, axis=-1, keepdims=True)
                gs = (probs * (gp - inner) * 0.125).astype(BF)
                results.append((dot(gs, k, NN), dot(gs, q, TN), dot(rough, gc, TN), dot(rough, v, NN)))
            for t in range(4):
                both = jnp.where(low, results[0][t], results[1][t])
                back[t, :, :, part] = both.astype(BF).reshape(CB, FG, 128)

        for t in range(4):
            exchange(back, home, bsend, brecv, t, c)

    for t in range(3):
        for c in range(2):
            arrived(home, brecv, t, c)

        @pl.loop(0, 4)
        def _(i):
            part = pl.ds(pl.multiple_of(i * 256, 256), 256)
            tile = dot(home[t].reshape(FR, D), w[3 - t, i].reshape(256, D), NT)
            gn[:, part] = tile if t == 0 else gn[:, part] + tile

    @pl.loop(0, 8)
    def _(i):
        rows = pl.ds(pl.multiple_of(i * 32, 32), 32)
        wide = x_ref[rows, :].astype(F32)
        r = lax.rsqrt(jnp.mean(wide * wide, axis=-1, keepdims=True) + EPS)
        s = gn[rows, :] * gain_ref[...]
        inner = jnp.mean(s * wide, axis=-1, keepdims=True)
        gin_ref[rows, :] = (g_ref[rows, :].astype(F32) + r * (s - wide * (r * r * inner))).astype(BF)

    for c in range(2):
        arrived(home, brecv, 3, c)

    @pl.loop(0, 4)
    def _(i):
        part = pl.ds(pl.multiple_of(i * 256, 256), 256)
        tile = dot(home[3].reshape(FR, D), w[0, :, :, :, part].reshape(D, 256), NN)
        out_ref[:, part] = (x_ref[:, part].astype(F32) + tile).astype(BF)

    for p in range(4):
        for s in range(17):
            copies[p, s].wait_send()
        for c in range(2):
            sent(fwd, fsend, p, c)
            sent(back, bsend, p, c)


def body(inputs, norm_gain, w_qkv, w_out, grad_out):
    vmem = pl.BlockSpec(memory_space=pltpu.VMEM)
    block = (4, CB, FG, D)
    outputs, grad_in = pl.pallas_call(
        kernel,
        out_shape=[jax.ShapeDtypeStruct((FR, D), BF)] * 2,
        in_specs=[vmem] * 5,
        out_specs=[vmem] * 2,
        scratch_shapes=[
            pltpu.VMEM((4, 4, 4, 64, D), BF),
            pltpu.VMEM((FR, D), BF),
            pltpu.VMEM(block, BF),
            pltpu.VMEM(block, BF),
            pltpu.VMEM(block, BF),
            pltpu.VMEM(block, BF),
            pltpu.VMEM((FR, D), F32),
            pltpu.SemaphoreType.DMA((4, 17)),
            pltpu.SemaphoreType.DMA((4, 17)),
            pltpu.SemaphoreType.DMA((4,)),
            pltpu.SemaphoreType.DMA((4, 2)),
            pltpu.SemaphoreType.DMA((4, 2)),
            pltpu.SemaphoreType.DMA((4, 2)),
            pltpu.SemaphoreType.DMA((4, 2)),
        ],
        compiler_params=pltpu.CompilerParams(
            collective_id=0, has_side_effects=True, vmem_limit_bytes=60 * 2**20
        ),
    )(
        inputs.reshape(FR, D),
        norm_gain.reshape(1, D),
        w_qkv.reshape(32, 3 * D),
        w_out.reshape(32, D),
        grad_out.reshape(FR, D),
    )
    return outputs.reshape(FR, 1, D), grad_in.reshape(FR, 1, D)


def solution(mesh):
    return jax.shard_map(
        body,
        mesh=mesh,
        in_specs=(
            P("frame", "cb", None),
            P(),
            P("cb", "frame", None),
            P("cb", "frame", None),
            P("frame", "cb", None),
        ),
        out_specs=(P("frame", "cb", None), P("frame", "cb", None)),
        check_vma=False,
    )
```

time: 613 us -> 235 us (0.38)
  waiting for transfers between devices: 474 us -> 0 us
  Pallas kernels: 0 us -> 231 us
  starting transfers between devices: 53.3 us -> 0 us
  matrix products: 39.4 us -> 0 us
  local copies, waits for them, and re-layouts: 25.1 us -> 2.72 us
  between operations: 14.3 us -> 0.65 us
    all_gather x2 -> x0, waiting for transfers between devices: 343 us -> none  [the longest x1 204 us: body(): lax.all_gather(w_qkv, 'frame', axis=1, tiled=True)]
    pallas_call x0 -> x1, Pallas kernels: none -> 231 us  [body(): pl.pallas_call(kernel, out_shape=[jax.ShapeDtypeStruct((FR, D), BF)] * 2,...]
    all_to_all x8 -> x0, waiting for transfers between devices: 129 us -> none  [the longest x1 24.1 us: body(): lax.all_to_all(key_rows, 'cb', split_axis=0, concat_axis=1, tiled=True)]
    all_to_all x8 -> x0, starting transfers between devices: 53.2 us -> none  [the longest x1 7.06 us: body(): lax.all_to_all(values, 'cb', split_axis=0, concat_axis=1, tiled=True)]
    dot_general x9 -> x0, matrix products: 34.5 us -> none  [the longest x1 5.92 us: attention_grads(): jnp.einsum('fhij,fjhe->fihe', grad_scores, to_heads(key_rows, head_count)...]
    convert_element_type x8 -> x0, local copies, waits for them, and re-layouts: 9.67 us -> none  [the longest x2 3.1 us: attention_grads(): grad_keys.reshape(shape_full).astype(jnp.bfloat16)]
    unnamed x31 -> x4, local copies, waits for them, and re-layouts: 11.1 us -> 2.72 us
  transfers between devices with their start and end apart: 10 -> 0, of which waited for: 9 -> 0; matrix products, arithmetic and copies ran while one was open for 11% -> 0% of each run, Pallas kernels for 0% -> 0%
where the time goes in v1:
time: 235 us; the launch traced here: 234 us
  Pallas kernels  231 us (98%)
  local copies, waits for them, and re-layouts  2.72 us (1%)
    pallas_call x1, Pallas kernels, body(): pl.pallas_call(kernel, out_shape=[jax.ShapeDtypeStruct((FR, D), BF)] * 2,...  231 us

profile of v1, /device:TPU:1, one launch (start us, length us, event | category | flops | bytes accessed | tf_op | source)
XLA Modules:
  0.0 234.0 jit_solution(6491193545771037702)
XLA Ops:
  0.6 230.6 %shard_map.68 = (bf16[256,1024]{1,0:T(8,128)(2,1)}, bf16[256,1024]{1,0:T(8,128)(2,1)}) custom-call(bf16[256,1024]{1,0:T(8,128)(2,1)} %bitcast.7, f32[1,1024]{1,0:T(1,128)} %bitcast.13, bf16[32,3072]{1,0:T(8,128)(2,1)} %bitcast.11, bf16[32,1024]{1,0:T(8,128)(2,1)} %bitcast.12, bf16[256,1024]{1,0:T(8,128)(2,1)} %bitcast.8), custom_call_target="tpu_custom_call" | custom-call | tf_op jit(solution)/shard_map/pallas_call | solution.py:256
  231.3 0.0 copy-start
  231.3 1.9 copy.9
  233.2 0.0 copy-done
  233.2 0.8 copy.10
Async XLA Ops:
  231.3 1.9 copy-start

commit v2 on v1

v2 whole, which is shorter than its diff:
```python
import functools

import jax
import jax.numpy as jnp
from jax import lax
from jax.experimental import pallas as pl
from jax.experimental.pallas import tpu as pltpu
from jax.sharding import PartitionSpec as P

D = 1024
CB = 16
FR = 256
GR = 8
FG = FR // GR
CH = 256
NCH = D // CH
EPS = 1e-05
BF = jnp.bfloat16
F32 = jnp.float32
NT = (((1,), (1,)), ((), ()))
NN = (((1,), (0,)), ((), ()))
TN = (((0,), (0,)), ((), ()))


def dot(a, b, dims):
    return lax.dot_general(a, b, dims, preferred_element_type=F32)


def kernel(
    x_hbm, gain_ref, wqkv_ref, wout_ref, g_hbm, out_ref, gin_ref,
    x_ref, g_ref, w, normed, fwd, got, gotx, back, backx, home, homex, gn, total,
    zsend, zrecv, gsend, grecv, lsem, isem, fsend, frecv, fxsend, fxrecv, bsend, brecv, bxsend, bxrecv,
):
    cb = lax.axis_index("cb")
    fr = lax.axis_index("frame")
    upper, me = cb // GR, cb % GR
    x, y, zh = fr // 8, (fr // 2) % 4, fr % 2
    xr, xl = (x + 1) % 4, (x + 3) % 4
    yr, yl = (y + 1) % 4, (y + 3) % 4

    def at(xx, yy, zz):
        return {"frame": (xx * 4 + yy) * 2 + zz}

    loads = [
        pltpu.make_async_copy(x_hbm, x_ref, isem.at[0]),
        pltpu.make_async_copy(g_hbm, g_ref, isem.at[1]),
    ]
    for load in loads:
        load.start()

    barrier = pltpu.get_barrier_semaphore()
    for peer in (at(x, y, 1 - zh), at(xr, y, zh), at(xl, y, zh), at(x, yr, zh), at(x, yl, zh)):
        pl.semaphore_signal(barrier, inc=1, device_id=peer)

    @pl.loop(1, CB)
    def _(j):
        pl.semaphore_signal(barrier, inc=1, device_id={"cb": (cb + j) % CB})

    ways_x, ways_y = (at(xr, y, zh), at(xl, y, zh)), (at(x, yr, zh), at(x, yl, zh))
    copies = {}

    def keep(m):
        shard = wqkv_ref.at[:, pl.ds((3 - m) * D, D)] if m else wout_ref
        local = pltpu.make_async_copy(shard, w.at[m, x, y, pl.ds(zh * 32, 32), :], lsem.at[m])
        local.start()
        copies[m] = local

    def swap(m, j):
        key = 0 if m == 0 else 1 + 3 * j + m - 1
        width = CH if m else D
        copy = pltpu.make_async_remote_copy(
            src_ref=wqkv_ref.at[:, pl.ds((3 - m) * D + j * CH, CH)] if m else wout_ref,
            dst_ref=w.at[m, x, y, pl.ds(zh * 32, 32), pl.ds(j * CH, width)],
            send_sem=zsend.at[key], recv_sem=zrecv.at[key],
            device_id=at(x, y, 1 - zh), device_id_type=pl.DeviceIdType.MESH,
        )
        copy.start()
        copies["z", m, j] = copy

    def remote(key, src, dst, peer):
        copy = pltpu.make_async_remote_copy(
            src_ref=src, dst_ref=dst, send_sem=gsend.at[key], recv_sem=grecv.at[key],
            device_id=peer, device_id_type=pl.DeviceIdType.MESH,
        )
        copy.start()
        copies[key] = copy

    def view(p, h, xs, ys, half=None):
        if p in (0, 5):
            start = 32 * (zh if p == 0 else 1 - zh)
            rows = pl.ds(start, 32) if half is None else pl.ds(start + 16 * half, 16)
            return w.at[0, xs, ys, rows, pl.ds(h * 512, 512)]
        rows = slice(None) if half is None else pl.ds(32 * half, 32)
        return w.at[pl.ds(1, 3), xs, ys, rows, pl.ds((p - 1) * CH + h * 128, 128)]

    def landed(j):
        for m in (1, 2, 3):
            if j == 0:
                copies[m].wait()
            copies["z", m, j].wait_recv()

    def tick0(p):
        for h, ways in ((0, ways_x), (1, ways_y)):
            block = view(p, h, x, y)
            remote((p, 1 + 4 * h), block, block, ways[0])
            remote((p, 2 + 4 * h), block, block, ways[1])

    def tick1(p):
        for h, ways in ((0, ways_x), (1, ways_y)):
            copies[p, 1 + 4 * h].wait_recv()
            block = view(p, h, *((xl, y), (x, yl))[h], 0)
            remote((p, 3 + 4 * h), block, block, ways[0])
        for h, ways in ((0, ways_x), (1, ways_y)):
            copies[p, 2 + 4 * h].wait_recv()
            block = view(p, h, *((xr, y), (x, yr))[h], 1)
            remote((p, 4 + 4 * h), block, block, ways[1])

    def line(p, h, pos, span):
        return view(p, h, *((span, pos), (pos, span))[h])

    def tick2(p):
        for h, ways in ((0, ways_y), (1, ways_x)):
            copies[p, 3 + 4 * h].wait_recv()
            copies[p, 4 + 4 * h].wait_recv()
            block = line(p, h, (y, x)[h], slice(None))
            remote((p, 9 + 4 * h), block, block, ways[0])
            remote((p, 10 + 4 * h), block, block, ways[1])

    def tick3(p):
        for h, ways in ((0, ways_y), (1, ways_x)):
            copies[p, 9 + 4 * h].wait_recv()
            block = line(p, h, (yl, xl)[h], pl.ds(0, 2))
            remote((p, 11 + 4 * h), block, block, ways[0])
        for h, ways in ((0, ways_y), (1, ways_x)):
            copies[p, 10 + 4 * h].wait_recv()
            block = line(p, h, (yr, xr)[h], pl.ds(2, 2))
            remote((p, 12 + 4 * h), block, block, ways[1])

    def tick4(p):
        for s in (11, 12, 15, 16):
            copies[p, s].wait_recv()

    def chunk(j):
        return pl.ds(j * CH, CH)

    def exchange(src, dst, ssem, rsem, t, j, way=None):
        @pl.loop(0, GR)
        def _(i):
            peer = (me + 4 + i) % GR
            wanted = {None: peer != me, 0: peer < me, 1: peer > me}[way]

            @pl.when(wanted)
            def _():
                pltpu.make_async_remote_copy(
                    src_ref=src.at[t, j, peer], dst_ref=dst.at[t, j, me],
                    send_sem=ssem.at[t, j], recv_sem=rsem.at[t, j],
                    device_id={"cb": upper * GR + peer}, device_id_type=pl.DeviceIdType.MESH,
                ).start()

        if way != 1:
            pltpu.make_async_copy(src.at[t, j, me], dst.at[t, j, me], rsem.at[t, j]).start()

    def across(src, dst, ssem, rsem, t, t2, j):
        @pl.loop(0, GR)
        def _(i):
            peer = (me + 4 + i) % GR
            pltpu.make_async_remote_copy(
                src_ref=src.at[t, j, peer], dst_ref=dst.at[t2, j, me],
                send_sem=ssem.at[t2, j], recv_sem=rsem.at[t2, j],
                device_id={"cb": (1 - upper) * GR + peer}, device_id_type=pl.DeviceIdType.MESH,
            ).start()

    def drain(buf, sem, t, j, count=GR):
        whole = buf.at[t, j, pl.ds(0, count)]
        pltpu.make_async_copy(whole, whole, sem.at[t, j]).wait()

    def project(m, j):
        if m == 0:
            tile = dot(g_ref[...], w[0, j].reshape(CH, D), NT)
        else:
            tile = dot(normed[...], w[m, :, :, :, chunk(j)].reshape(D, CH), NN)
        fwd[m, j] = tile.astype(BF).reshape(GR, FG, CH)

        if m in (1, 2):
            @pl.when(upper == 0)
            def _():
                across(fwd, gotx, fxsend, fxrecv, m, m - 1, j)

        exchange(fwd, got, fsend, frecv, m, j)

    def projections(j):
        for m in (1, 2, 3):
            project(m, j)

    ri = lax.broadcasted_iota(jnp.int32, (FR, FR), 0)
    ci = lax.broadcasted_iota(jnp.int32, (FR, FR), 1)
    low = lax.broadcasted_iota(jnp.int32, (FR, 128), 1) < 64
    zero = jnp.zeros((FR, 128), BF)

    def heads(j, wide):
        @pl.loop(0, 2)
        def _(i):
            part = pl.ds(pl.multiple_of(i * 128, 128), 128)
            frame = (ri & (FG - 1)) == (ci & (FG - 1))
            masks = [jnp.logical_and(frame, ri >= ci)]
            gc, v, k, q = (got[t, j, :, :, part].reshape(FR, 128) for t in range(4))
            vs, ks = [v], [k]
            if wide:
                masks.append(frame)
                vs.append(gotx[0, j, :, :, part].reshape(FR, 128))
                ks.append(gotx[1, j, :, :, part].reshape(FR, 128))
            results = []
            for mine in (low, jnp.logical_not(low)):
                q1, gc1 = jnp.where(mine, q, zero), jnp.where(mine, gc, zero)
                scores = [
                    jnp.where(seen, dot(q1, kk, NT) * 0.125, -jnp.inf) for seen, kk in zip(masks, ks)
                ]
                top = functools.reduce(jnp.maximum, [jnp.max(s, axis=-1, keepdims=True) for s in scores])
                e = [jnp.exp(s - top) for s in scores]
                norm = sum(jnp.sum(s, axis=-1, keepdims=True) for s in e)
                probs = [s / norm for s in e]
                rough = [s.astype(BF) for s in probs]
                gp = [dot(gc1, vv, NT) for vv in vs]
                inner = sum(jnp.sum(a * b, axis=-1, keepdims=True) for a, b in zip(probs, gp))
                gs = [(a * (b - inner) * 0.125).astype(BF) for a, b in zip(probs, gp)]
                found = [
                    sum(dot(a, b, NN) for a, b in zip(gs, ks)),
                    dot(gs[0], q, TN),
                    dot(rough[0], gc, TN),
                    sum(dot(a, b, NN) for a, b in zip(rough, vs)),
                ]
                if wide:
                    found += [dot(gs[1], q, TN), dot(rough[1], gc, TN)]
                results.append(found)
            for t, (a, b) in enumerate(zip(*results)):
                both = jnp.where(low, a, b).astype(BF).reshape(GR, FG, 128)
                if t < 4:
                    back[t, j, :, :, part] = both
                else:
                    backx[t - 4, j, :, :, part] = both

    def attend(j):
        for t in range(4):
            drain(got, frecv, t, j)

        @pl.when(upper == 0)
        def _():
            heads(j, False)

        @pl.when(upper == 1)
        def _():
            for t in range(2):
                drain(gotx, fxrecv, t, j)
            heads(j, True)
            for t in range(2):
                across(backx, homex, bxsend, bxrecv, t, t, j)

        for t in range(4):
            exchange(back, home, bsend, brecv, t, j, 0)

    def finish(j):
        for t in range(3):
            drain(home, brecv, t, j)

        @pl.when(upper == 0)
        def _():
            for t in range(2):
                drain(homex, bxrecv, t, j)
                home[t + 1, j] = (home[t + 1, j].astype(F32) + homex[t, j].astype(F32)).astype(BF)

        @pl.loop(0, 4)
        def _(i):
            part = pl.ds(pl.multiple_of(i * 256, 256), 256)
            tile = sum(
                dot(home[t, j].reshape(FR, CH), w[3 - t, i, :, :, chunk(j)].reshape(256, CH), NT)
                for t in range(3)
            )
            gn[:, part] = tile if j == 0 else gn[:, part] + tile

        if j == NCH - 1:
            @pl.loop(0, 8)
            def _(i):
                rows = pl.ds(pl.multiple_of(i * 32, 32), 32)
                wide = x_ref[rows, :].astype(F32)
                r = lax.rsqrt(jnp.mean(wide * wide, axis=-1, keepdims=True) + EPS)
                s = gn[rows, :] * gain_ref[...]
                inner = jnp.mean(s * wide, axis=-1, keepdims=True)
                gin_ref[rows, :] = (
                    g_ref[rows, :].astype(F32) + r * (s - wide * (r * r * inner))
                ).astype(BF)

        drain(home, brecv, 3, j)

        @pl.loop(0, 4)
        def _(i):
            part = pl.ds(pl.multiple_of(i * 256, 256), 256)
            tile = dot(
                home[3, j].reshape(FR, CH), w[0, j, :, :, part].reshape(CH, 256), NN
            )
            tile = tile + (x_ref[:, part].astype(F32) if j == 0 else total[:, part])
            if j == NCH - 1:
                out_ref[:, part] = tile.astype(BF)
            else:
                total[:, part] = tile

    for m in range(4):
        keep(m)

    loads[0].wait()

    @pl.loop(0, 8)
    def _(i):
        rows = pl.ds(pl.multiple_of(i * 32, 32), 32)
        wide = x_ref[rows, :].astype(F32)
        r = lax.rsqrt(jnp.mean(wide * wide, axis=-1, keepdims=True) + EPS)
        normed[rows, :] = (wide * r * gain_ref[...]).astype(BF)

    loads[1].wait()
    copies[0].wait()
    pl.semaphore_wait(barrier, 5 + CB - 1)

    swap(0, 0)
    tick0(0)
    for m in (1, 2, 3):
        swap(m, 0)
    tick1(0)
    copies["z", 0, 0].wait_recv()
    tick0(5), tick2(0), tick1(5), tick3(0), tick2(5)
    for j in range(1, NCH):
        for m in (1, 2, 3):
            swap(m, j)
    landed(0)
    tick0(1), tick4(0), tick3(5), tick1(1), tick4(5)
    for j in range(NCH):
        project(0, j)
    tick2(1), landed(1), tick0(2), tick3(1), tick1(2), tick4(1)
    projections(0)
    tick2(2), landed(2), tick0(3), tick3(2), tick1(3), tick4(2)
    projections(1)
    tick2(3), landed(3), tick0(4), tick3(3), tick1(4), tick4(3)
    projections(2)
    tick2(4), tick3(4), tick4(4)
    projections(3)
    attend(0)
    attend(1)
    attend(2)
    attend(3)
    for j in range(NCH):
        for t in range(4):
            exchange(back, home, bsend, brecv, t, j, 1)
    finish(0)
    finish(1)
    finish(2)
    finish(3)

    copies["z", 0, 0].wait_send()
    for m in range(4):
        for j in range(NCH):
            if m:
                copies["z", m, j].wait_send()
            drain(fwd, fsend, m, j, GR - 1)
            drain(back, bsend, m, j, GR - 1)
    for p in range(2 + NCH):
        for s in range(1, 17):
            copies[p, s].wait_send()

    @pl.when(upper == 0)
    def _():
        for t in range(2):
            for j in range(NCH):
                drain(gotx, fxsend, t, j)

    @pl.when(upper == 1)
    def _():
        for t in range(2):
            for j in range(NCH):
                drain(homex, bxsend, t, j)


def body(inputs, norm_gain, w_qkv, w_out, grad_out):
    vmem, hbm = pl.BlockSpec(memory_space=pltpu.VMEM), pl.BlockSpec(memory_space=pl.ANY)
    four, two = pltpu.VMEM((4, NCH, GR, FG, CH), BF), pltpu.VMEM((2, NCH, GR, FG, CH), BF)
    sem4, sem2 = pltpu.SemaphoreType.DMA((4, NCH)), pltpu.SemaphoreType.DMA((2, NCH))
    outputs, grad_in = pl.pallas_call(
        kernel,
        out_shape=[jax.ShapeDtypeStruct((FR, D), BF)] * 2,
        in_specs=[hbm, vmem, hbm, hbm, hbm],
        out_specs=[vmem] * 2,
        scratch_shapes=[
            pltpu.VMEM((FR, D), BF),
            pltpu.VMEM((FR, D), BF),
            pltpu.VMEM((4, 4, 4, 64, D), BF),
            pltpu.VMEM((FR, D), BF),
            four, four, two, four, two, four, two,
            pltpu.VMEM((FR, D), F32),
            pltpu.VMEM((FR, D), F32),
            pltpu.SemaphoreType.DMA((1 + 3 * NCH,)),
            pltpu.SemaphoreType.DMA((1 + 3 * NCH,)),
            pltpu.SemaphoreType.DMA((2 + NCH, 17)),
            pltpu.SemaphoreType.DMA((2 + NCH, 17)),
            pltpu.SemaphoreType.DMA((4,)),
            pltpu.SemaphoreType.DMA((2,)),
            sem4, sem4, sem2, sem2, sem4, sem4, sem2, sem2,
        ],
        compiler_params=pltpu.CompilerParams(
            collective_id=0, has_side_effects=True, vmem_limit_bytes=60 * 2**20
        ),
    )(
        inputs.reshape(FR, D),
        norm_gain.reshape(1, D),
        w_qkv.reshape(32, 3 * D),
        w_out.reshape(32, D),
        grad_out.reshape(FR, D),
    )
    return outputs.reshape(FR, 1, D), grad_in.reshape(FR, 1, D)


def solution(mesh):
    return jax.shard_map(
        body,
        mesh=mesh,
        in_specs=(
            P("frame", "cb", None),
            P(),
            P("cb", "frame", None),
            P("cb", "frame", None),
            P("frame", "cb", None),
        ),
        out_specs=(P("frame", "cb", None), P("frame", "cb", None)),
        check_vma=False,
    )
```

time: 235 us -> 221 us (0.940)
  Pallas kernels: 231 us -> 218 us
    pallas_call x1, Pallas kernels: 231 us -> 218 us  [body(): pl.pallas_call(kernel, out_shape=[jax.ShapeDtypeStruct((FR, D), BF)] * 2,...]
where the time goes in v2:
time: 221 us
  Pallas kernels  218 us (99%)
  local copies, waits for them, and re-layouts  2.72 us (1%)
    pallas_call x1, Pallas kernels, body(): pl.pallas_call(kernel, out_shape=[jax.ShapeDtypeStruct((FR, D), BF)] * 2,...  218 us

profile of v2, /device:TPU:1, one launch (start us, length us, event | category | flops | bytes accessed | tf_op | source)
XLA Modules:
  0.0 221.2 jit_solution(14544691280928631113)
XLA Ops:
  0.6 217.8 %shard_map.68 = (bf16[256,1024]{1,0:T(8,128)(2,1)}, bf16[256,1024]{1,0:T(8,128)(2,1)}) custom-call(bf16[256,1024]{1,0:T(8,128)(2,1)} %bitcast.7, f32[1,1024]{1,0:T(1,128)} %bitcast.13, bf16[32,3072]{1,0:T(8,128)(2,1)} %bitcast.11, bf16[32,1024]{1,0:T(8,128)(2,1)} %bitcast.12, bf16[256,1024]{1,0:T(8,128)(2,1)} %bitcast.8), custom_call_target="tpu_custom_call" | custom-call | tf_op jit(solution)/shard_map/pallas_call | solution.py:384
  218.5 0.0 copy-start
  218.5 1.9 copy.9
  220.4 0.0 copy-done
  220.4 0.8 copy.10
Async XLA Ops:
  218.5 1.9 copy-start

commit v3 on v2

--- a/solution.py
+++ b/solution.py
@@ -14,6 +14,7 @@
 FG = FR // GR
 CH = 256
 NCH = D // CH
+LOW = 1
 EPS = 1e-05
 BF = jnp.bfloat16
 F32 = jnp.float32
@@ -28,8 +29,9 @@
 
 def kernel(
     x_hbm, gain_ref, wqkv_ref, wout_ref, g_hbm, out_ref, gin_ref,
-    x_ref, g_ref, w, normed, fwd, got, gotx, back, backx, home, homex, gn, total,
-    zsend, zrecv, gsend, grecv, lsem, isem, fsend, frecv, fxsend, fxrecv, bsend, brecv, bxsend, bxrecv,
+    x_ref, g_ref, w, normed, fwd, got, gotx, gotl, back, backx, backl, home, homex, gn, total,
+    zsend, zrecv, gsend, grecv, lsem, isem, fsend, frecv, fxsend, fxrecv, flsend, flrecv,
+    bsend, brecv, bxsend, bxrecv, blsend,
 ):
     cb = lax.axis_index("cb")
     fr = lax.axis_index("frame")
@@ -89,14 +91,14 @@
         if p in (0, 5):
             start = 32 * (zh if p == 0 else 1 - zh)
             rows = pl.ds(start, 32) if half is None else pl.ds(start + 16 * half, 16)
+            return w.at[pl.ds(1, 3), xs, ys, rows, pl.ds(h * 128, 128)]
+        rows = slice(None) if half is None else pl.ds(32 * half, 32)
+        if p == 1:
             return w.at[0, xs, ys, rows, pl.ds(h * 512, 512)]
-        rows = slice(None) if half is None else pl.ds(32 * half, 32)
         return w.at[pl.ds(1, 3), xs, ys, rows, pl.ds((p - 1) * CH + h * 128, 128)]
 
     def landed(j):
         for m in (1, 2, 3):
-            if j == 0:
-                copies[m].wait()
             copies["z", m, j].wait_recv()
 
     def tick0(p):
@@ -160,19 +162,20 @@
         if way != 1:
             pltpu.make_async_copy(src.at[t, j, me], dst.at[t, j, me], rsem.at[t, j]).start()
 
-    def across(src, dst, ssem, rsem, t, t2, j):
+    def across(src, dst, ssem, rsem):
         @pl.loop(0, GR)
         def _(i):
             peer = (me + 4 + i) % GR
             pltpu.make_async_remote_copy(
-                src_ref=src.at[t, j, peer], dst_ref=dst.at[t2, j, me],
-                send_sem=ssem.at[t2, j], recv_sem=rsem.at[t2, j],
+                src_ref=src.at[peer], dst_ref=dst.at[me], send_sem=ssem, recv_sem=rsem,
                 device_id={"cb": (1 - upper) * GR + peer}, device_id_type=pl.DeviceIdType.MESH,
             ).start()
 
+    def wait(whole, sem):
+        pltpu.make_async_copy(whole, whole, sem).wait()
+
     def drain(buf, sem, t, j, count=GR):
-        whole = buf.at[t, j, pl.ds(0, count)]
-        pltpu.make_async_copy(whole, whole, sem.at[t, j]).wait()
+        wait(buf.at[t, j, pl.ds(0, count)], sem.at[t, j])
 
     def project(m, j):
         if m == 0:
@@ -182,11 +185,17 @@
         fwd[m, j] = tile.astype(BF).reshape(GR, FG, CH)
 
         if m in (1, 2):
-            @pl.when(upper == 0)
+            @pl.when(upper == int(j == LOW))
             def _():
-                across(fwd, gotx, fxsend, fxrecv, m, m - 1, j)
-
-        exchange(fwd, got, fsend, frecv, m, j)
+                across(fwd.at[m, j], gotx.at[m - 1, j], fxsend.at[m - 1, j], fxrecv.at[m - 1, j])
+        elif j == LOW:
+            @pl.when(upper == 1)
+            def _():
+                across(fwd.at[m, j], gotl.at[m // 3], flsend.at[m // 3], flrecv.at[m // 3])
+
+        @pl.when(jnp.logical_or(upper == 0, j != LOW))
+        def _():
+            exchange(fwd, got, fsend, frecv, m, j)
 
     def projections(j):
         for m in (1, 2, 3):
@@ -197,72 +206,116 @@
     low = lax.broadcasted_iota(jnp.int32, (FR, 128), 1) < 64
     zero = jnp.zeros((FR, 128), BF)
 
-    def heads(j, wide):
+    def grads(mine, masks, q, gc, ks, vs):
+        q1, gc1 = jnp.where(mine, q, zero), jnp.where(mine, gc, zero)
+        scores = [jnp.where(seen, dot(q1, k, NT) * 0.125, -jnp.inf) for seen, k in zip(masks, ks)]
+        top = functools.reduce(jnp.maximum, [jnp.max(s, axis=-1, keepdims=True) for s in scores])
+        e = [jnp.exp(s - top) for s in scores]
+        norm = sum(jnp.sum(s, axis=-1, keepdims=True) for s in e)
+        probs = [s / norm for s in e]
+        rough = [s.astype(BF) for s in probs]
+        gp = [dot(gc1, v, NT) for v in vs]
+        inner = sum(jnp.sum(a * b, axis=-1, keepdims=True) for a, b in zip(probs, gp))
+        gs = [(a * (b - inner) * 0.125).astype(BF) for a, b in zip(probs, gp)]
+        found = [
+            sum(dot(a, b, NN) for a, b in zip(gs, ks)),
+            dot(gs[0], q, TN),
+            dot(rough[0], gc, TN),
+            sum(dot(a, b, NN) for a, b in zip(rough, vs)),
+        ]
+        for a, b in zip(gs[1:], rough[1:]):
+            found += [dot(a, q, TN), dot(b, gc, TN)]
+        return found
+
+    def heads(j):
         @pl.loop(0, 2)
         def _(i):
             part = pl.ds(pl.multiple_of(i * 128, 128), 128)
             frame = (ri & (FG - 1)) == (ci & (FG - 1))
-            masks = [jnp.logical_and(frame, ri >= ci)]
-            gc, v, k, q = (got[t, j, :, :, part].reshape(FR, 128) for t in range(4))
-            vs, ks = [v], [k]
-            if wide:
-                masks.append(frame)
-                vs.append(gotx[0, j, :, :, part].reshape(FR, 128))
-                ks.append(gotx[1, j, :, :, part].reshape(FR, 128))
-            results = []
-            for mine in (low, jnp.logical_not(low)):
-                q1, gc1 = jnp.where(mine, q, zero), jnp.where(mine, gc, zero)
-                scores = [
-                    jnp.where(seen, dot(q1, kk, NT) * 0.125, -jnp.inf) for seen, kk in zip(masks, ks)
-                ]
-                top = functools.reduce(jnp.maximum, [jnp.max(s, axis=-1, keepdims=True) for s in scores])
-                e = [jnp.exp(s - top) for s in scores]
-                norm = sum(jnp.sum(s, axis=-1, keepdims=True) for s in e)
-                probs = [s / norm for s in e]
-                rough = [s.astype(BF) for s in probs]
-                gp = [dot(gc1, vv, NT) for vv in vs]
-                inner = sum(jnp.sum(a * b, axis=-1, keepdims=True) for a, b in zip(probs, gp))
-                gs = [(a * (b - inner) * 0.125).astype(BF) for a, b in zip(probs, gp)]
-                found = [
-                    sum(dot(a, b, NN) for a, b in zip(gs, ks)),
-                    dot(gs[0], q, TN),
-                    dot(rough[0], gc, TN),
-                    sum(dot(a, b, NN) for a, b in zip(rough, vs)),
-                ]
-                if wide:
-                    found += [dot(gs[1], q, TN), dot(rough[1], gc, TN)]
-                results.append(found)
-            for t, (a, b) in enumerate(zip(*results)):
-                both = jnp.where(low, a, b).astype(BF).reshape(GR, FG, 128)
-                if t < 4:
-                    back[t, j, :, :, part] = both
-                else:
-                    backx[t - 4, j, :, :, part] = both
+            causal = jnp.logical_and(frame, ri >= ci)
+
+            def load(*refs):
+                return [ref[:, :, part].reshape(FR, 128) for ref in refs]
+
+            def store(refs, results):
+                for ref, a, b in zip(refs, *results):
+                    ref[:, :, part] = jnp.where(low, a, b).astype(BF).reshape(GR, FG, 128)
+
+            sides = (low, jnp.logical_not(low))
+            backs = [back.at[t, j] for t in range(4)]
+
+            def apart(extra):
+                gc, v, k, q = load(*(got.at[t, j] for t in range(4)))
+                vs, ks, masks = [v], [k], [causal]
+                if extra:
+                    vx, kx = load(gotx.at[0, j], gotx.at[1, j])
+                    vs, ks, masks = [v, vx], [k, kx], [causal, frame]
+                store(
+                    backs + [backx.at[0, j], backx.at[1, j]] * extra,
+                    [grads(mine, masks, q, gc, ks, vs) for mine in sides],
+                )
+
+            def together():
+                gc, v, k, q = load(*(got.at[t, j] for t in range(4)))
+                vh, kh, gch, qh = load(gotx.at[0, j], gotx.at[1, j], gotl.at[0], gotl.at[1])
+                results = []
+                for mine in sides:
+                    a = grads(mine, [causal], q, gc, [k], [v])
+                    b = grads(mine, [causal, frame], qh, gch, [kh, k], [vh, v])
+                    results.append([a[0], a[1] + b[4], a[2] + b[5], a[3]] + b[:4])
+                store(backs + [backl.at[t] for t in range(4)], results)
+
+            if j == LOW:
+                together()
+            else:
+                @pl.when(upper == 0)
+                def _():
+                    apart(0)
+
+                @pl.when(upper == 1)
+                def _():
+                    apart(1)
 
     def attend(j):
-        for t in range(4):
-            drain(got, frecv, t, j)
-
+        @pl.when(jnp.logical_or(upper == 0, j != LOW))
+        def _():
+            for t in range(4):
+                drain(got, frecv, t, j)
+
+            @pl.when(upper == int(j != LOW))
+            def _():
+                for t in range(2):
+                    drain(gotx, fxrecv, t, j)
+                    if j == LOW:
+                        wait(gotl.at[t], flrecv.at[t])
+
+            heads(j)
+            if j != LOW:
+                @pl.when(upper == 1)
+                def _():
+                    for t in range(2):
+                        across(backx.at[t, j], homex.at[t, j], bxsend.at[t, j], bxrecv.at[t, j])
+
+            for t in range(4):
+                exchange(back, home, bsend, brecv, t, j, 0)
+
+    def rest(j):
+        @pl.when(jnp.logical_or(upper == 0, j != LOW))
+        def _():
+            for t in range(4):
+                exchange(back, home, bsend, brecv, t, j, 1)
+
+    def lift(ts):
         @pl.when(upper == 0)
         def _():
-            heads(j, False)
-
-        @pl.when(upper == 1)
-        def _():
-            for t in range(2):
-                drain(gotx, fxrecv, t, j)
-            heads(j, True)
-            for t in range(2):
-                across(backx, homex, bxsend, bxrecv, t, t, j)
-
-        for t in range(4):
-            exchange(back, home, bsend, brecv, t, j, 0)
-
-    def finish(j):
+            for t in ts:
+                across(backl.at[t], home.at[t, LOW], blsend.at[t], brecv.at[t, LOW])
+
+    def finish(j, first=False, last=False):
         for t in range(3):
             drain(home, brecv, t, j)
 
-        @pl.when(upper == 0)
+        @pl.when(jnp.logical_and(upper == 0, j != LOW))
         def _():
             for t in range(2):
                 drain(homex, bxrecv, t, j)
@@ -275,9 +328,9 @@
                 dot(home[t, j].reshape(FR, CH), w[3 - t, i, :, :, chunk(j)].reshape(256, CH), NT)
                 for t in range(3)
             )
-            gn[:, part] = tile if j == 0 else gn[:, part] + tile
-
-        if j == NCH - 1:
+            gn[:, part] = tile if first else gn[:, part] + tile
+
+        if last:
             @pl.loop(0, 8)
             def _(i):
                 rows = pl.ds(pl.multiple_of(i * 32, 32), 32)
@@ -297,13 +350,13 @@
             tile = dot(
                 home[3, j].reshape(FR, CH), w[0, j, :, :, part].reshape(CH, 256), NN
             )
-            tile = tile + (x_ref[:, part].astype(F32) if j == 0 else total[:, part])
-            if j == NCH - 1:
+            tile = tile + (x_ref[:, part].astype(F32) if first else total[:, part])
+            if last:
                 out_ref[:, part] = tile.astype(BF)
             else:
                 total[:, part] = tile
 
-    for m in range(4):
+    for m in (1, 2, 3, 0):
         keep(m)
 
     loads[0].wait()
@@ -315,26 +368,28 @@
         r = lax.rsqrt(jnp.mean(wide * wide, axis=-1, keepdims=True) + EPS)
         normed[rows, :] = (wide * r * gain_ref[...]).astype(BF)
 
-    loads[1].wait()
-    copies[0].wait()
+    for m in (1, 2, 3):
+        copies[m].wait()
     pl.semaphore_wait(barrier, 5 + CB - 1)
 
-    swap(0, 0)
-    tick0(0)
     for m in (1, 2, 3):
         swap(m, 0)
+    tick0(0)
+    swap(0, 0)
     tick1(0)
-    copies["z", 0, 0].wait_recv()
+    landed(0)
     tick0(5), tick2(0), tick1(5), tick3(0), tick2(5)
     for j in range(1, NCH):
         for m in (1, 2, 3):
             swap(m, j)
-    landed(0)
+    loads[1].wait()
+    copies[0].wait()
+    copies["z", 0, 0].wait_recv()
     tick0(1), tick4(0), tick3(5), tick1(1), tick4(5)
+    projections(0)
+    tick2(1), landed(1), tick0(2), tick3(1), tick1(2), tick4(1)
     for j in range(NCH):
         project(0, j)
-    tick2(1), landed(1), tick0(2), tick3(1), tick1(2), tick4(1)
-    projections(0)
     tick2(2), landed(2), tick0(3), tick3(2), tick1(3), tick4(2)
     projections(1)
     tick2(3), landed(3), tick0(4), tick3(3), tick1(4), tick4(3)
@@ -343,38 +398,51 @@
     projections(3)
     attend(0)
     attend(1)
+    lift((0, 1))
     attend(2)
+    lift((2, 3))
     attend(3)
+    order = [j for j in range(NCH) if j != LOW] + [LOW]
+    for j in order:
+        rest(j)
+    for j in order:
+        finish(j, j == order[0], j == order[-1])
+
+    copies["z", 0, 0].wait_send()
     for j in range(NCH):
-        for t in range(4):
-            exchange(back, home, bsend, brecv, t, j, 1)
-    finish(0)
-    finish(1)
-    finish(2)
-    finish(3)
-
-    copies["z", 0, 0].wait_send()
-    for m in range(4):
-        for j in range(NCH):
-            if m:
-                copies["z", m, j].wait_send()
-            drain(fwd, fsend, m, j, GR - 1)
-            drain(back, bsend, m, j, GR - 1)
+        for m in (1, 2, 3):
+            copies["z", m, j].wait_send()
+
+        @pl.when(jnp.logical_or(upper == 0, j != LOW))
+        def _():
+            for t in range(4):
+                drain(fwd, fsend, t, j, GR - 1)
+                drain(back, bsend, t, j, GR - 1)
+
+        @pl.when(upper == int(j == LOW))
+        def _():
+            for t in range(2):
+                drain(gotx, fxsend, t, j)
+
+        if j != LOW:
+            @pl.when(upper == 1)
+            def _():
+                for t in range(2):
+                    drain(homex, bxsend, t, j)
+
     for p in range(2 + NCH):
         for s in range(1, 17):
             copies[p, s].wait_send()
 
     @pl.when(upper == 0)
     def _():
-        for t in range(2):
-            for j in range(NCH):
-                drain(gotx, fxsend, t, j)
+        for t in range(4):
+            wait(backl.at[t], blsend.at[t])
 
     @pl.when(upper == 1)
     def _():
         for t in range(2):
-            for j in range(NCH):
-                drain(homex, bxsend, t, j)
+            wait(gotl.at[t], flsend.at[t])
 
 
 def body(inputs, norm_gain, w_qkv, w_out, grad_out):
@@ -391,7 +459,8 @@
             pltpu.VMEM((FR, D), BF),
             pltpu.VMEM((4, 4, 4, 64, D), BF),
             pltpu.VMEM((FR, D), BF),
-            four, four, two, four, two, four, two,
+            four, four, two, pltpu.VMEM((2, GR, FG, CH), BF), four, two,
+            pltpu.VMEM((4, GR, FG, CH), BF), four, two,
             pltpu.VMEM((FR, D), F32),
             pltpu.VMEM((FR, D), F32),
             pltpu.SemaphoreType.DMA((1 + 3 * NCH,)),
@@ -400,7 +469,11 @@
             pltpu.SemaphoreType.DMA((2 + NCH, 17)),
             pltpu.SemaphoreType.DMA((4,)),
             pltpu.SemaphoreType.DMA((2,)),
-            sem4, sem4, sem2, sem2, sem4, sem4, sem2, sem2,
+            sem4, sem4, sem2, sem2,
+            pltpu.SemaphoreType.DMA((2,)),
+            pltpu.SemaphoreType.DMA((2,)),
+            sem4, sem4, sem2, sem2,
+            pltpu.SemaphoreType.DMA((4,)),
         ],
         compiler_params=pltpu.CompilerParams(
             collective_id=0, has_side_effects=True, vmem_limit_bytes=60 * 2**20

time: 221 us -> 209 us (0.946)
  Pallas kernels: 218 us -> 205 us
    pallas_call x1, Pallas kernels: 218 us -> 205 us  [body(): pl.pallas_call(kernel, out_shape=[jax.ShapeDtypeStruct((FR, D), BF)] * 2,...]
where the time goes in v3:
time: 209 us
  Pallas kernels  205 us (98%)
  local copies, waits for them, and re-layouts  2.72 us (1%)
    pallas_call x1, Pallas kernels, body(): pl.pallas_call(kernel, out_shape=[jax.ShapeDtypeStruct((FR, D), BF)] * 2,...  205 us

profile of v3, /device:TPU:1, one launch (start us, length us, event | category | flops | bytes accessed | tf_op | source)
XLA Modules:
  0.0 208.7 jit_solution(17045814261911373445)
XLA Ops:
  0.6 205.3 %shard_map.68 = (bf16[256,1024]{1,0:T(8,128)(2,1)}, bf16[256,1024]{1,0:T(8,128)(2,1)}) custom-call(bf16[256,1024]{1,0:T(8,128)(2,1)} %bitcast.7, f32[1,1024]{1,0:T(1,128)} %bitcast.13, bf16[32,3072]{1,0:T(8,128)(2,1)} %bitcast.11, bf16[32,1024]{1,0:T(8,128)(2,1)} %bitcast.12, bf16[256,1024]{1,0:T(8,128)(2,1)} %bitcast.8), custom_call_target="tpu_custom_call" | custom-call | tf_op jit(solution)/shard_map/pallas_call | solution.py:452
  205.9 0.0 copy-start
  205.9 1.9 copy.9
  207.9 0.0 copy-done
  207.9 0.8 copy.10
Async XLA Ops:
  205.9 1.9 copy-start

commit v4 on v3

--- a/solution.py
+++ b/solution.py
@@ -12,9 +12,11 @@
 FR = 256
 GR = 8
 FG = FR // GR
-CH = 256
+CH = 128
 NCH = D // CH
-LOW = 1
+GC = 256
+NG = D // GC
+LOW = 2
 EPS = 1e-05
 BF = jnp.bfloat16
 F32 = jnp.float32
@@ -69,10 +71,10 @@
 
     def swap(m, j):
         key = 0 if m == 0 else 1 + 3 * j + m - 1
-        width = CH if m else D
+        width = GC if m else D
         copy = pltpu.make_async_remote_copy(
-            src_ref=wqkv_ref.at[:, pl.ds((3 - m) * D + j * CH, CH)] if m else wout_ref,
-            dst_ref=w.at[m, x, y, pl.ds(zh * 32, 32), pl.ds(j * CH, width)],
+            src_ref=wqkv_ref.at[:, pl.ds((3 - m) * D + j * GC, GC)] if m else wout_ref,
+            dst_ref=w.at[m, x, y, pl.ds(zh * 32, 32), pl.ds(j * GC, width)],
             send_sem=zsend.at[key], recv_sem=zrecv.at[key],
             device_id=at(x, y, 1 - zh), device_id_type=pl.DeviceIdType.MESH,
         )
@@ -95,7 +97,7 @@
         rows = slice(None) if half is None else pl.ds(32 * half, 32)
         if p == 1:
             return w.at[0, xs, ys, rows, pl.ds(h * 512, 512)]
-        return w.at[pl.ds(1, 3), xs, ys, rows, pl.ds((p - 1) * CH + h * 128, 128)]
+        return w.at[pl.ds(1, 3), xs, ys, rows, pl.ds((p - 1) * GC + h * 128, 128)]
 
     def landed(j):
         for m in (1, 2, 3):
@@ -177,9 +179,12 @@
     def drain(buf, sem, t, j, count=GR):
         wait(buf.at[t, j, pl.ds(0, count)], sem.at[t, j])
 
+    def out_rows(j, part):
+        return w[0, j // 2, pl.ds(j % 2 * 2, 2), :, part].reshape(CH, -1)
+
     def project(m, j):
         if m == 0:
-            tile = dot(g_ref[...], w[0, j].reshape(CH, D), NT)
+            tile = dot(g_ref[...], out_rows(j, slice(None)), NT)
         else:
             tile = dot(normed[...], w[m, :, :, :, chunk(j)].reshape(D, CH), NN)
         fwd[m, j] = tile.astype(BF).reshape(GR, FG, CH)
@@ -197,9 +202,10 @@
         def _():
             exchange(fwd, got, fsend, frecv, m, j)
 
-    def projections(j):
-        for m in (1, 2, 3):
-            project(m, j)
+    def projections(g):
+        for j in (2 * g, 2 * g + 1):
+            for m in (1, 2, 3):
+                project(m, j)
 
     ri = lax.broadcasted_iota(jnp.int32, (FR, FR), 0)
     ci = lax.broadcasted_iota(jnp.int32, (FR, FR), 1)
@@ -228,7 +234,7 @@
         return found
 
     def heads(j):
-        @pl.loop(0, 2)
+        @pl.loop(0, CH // 128)
         def _(i):
             part = pl.ds(pl.multiple_of(i * 128, 128), 128)
             frame = (ri & (FG - 1)) == (ci & (FG - 1))
@@ -265,16 +271,9 @@
                     results.append([a[0], a[1] + b[4], a[2] + b[5], a[3]] + b[:4])
                 store(backs + [backl.at[t] for t in range(4)], results)
 
-            if j == LOW:
-                together()
-            else:
-                @pl.when(upper == 0)
-                def _():
-                    apart(0)
-
-                @pl.when(upper == 1)
-                def _():
-                    apart(1)
+            pl.when(j == LOW)(together)
+            pl.when(jnp.logical_and(j != LOW, upper == 0))(lambda: apart(0))
+            pl.when(jnp.logical_and(j != LOW, upper == 1))(lambda: apart(1))
 
     def attend(j):
         @pl.when(jnp.logical_or(upper == 0, j != LOW))
@@ -282,19 +281,22 @@
             for t in range(4):
                 drain(got, frecv, t, j)
 
-            @pl.when(upper == int(j != LOW))
+            @pl.when(jnp.logical_or(upper == 1, j == LOW))
             def _():
                 for t in range(2):
                     drain(gotx, fxrecv, t, j)
-                    if j == LOW:
-                        wait(gotl.at[t], flrecv.at[t])
+
+            @pl.when(j == LOW)
+            def _():
+                for t in range(2):
+                    wait(gotl.at[t], flrecv.at[t])
 
             heads(j)
-            if j != LOW:
-                @pl.when(upper == 1)
-                def _():
-                    for t in range(2):
-                        across(backx.at[t, j], homex.at[t, j], bxsend.at[t, j], bxrecv.at[t, j])
+
+            @pl.when(upper == 1)
+            def _():
+                for t in range(2):
+                    across(backx.at[t, j], homex.at[t, j], bxsend.at[t, j], bxrecv.at[t, j])
 
             for t in range(4):
                 exchange(back, home, bsend, brecv, t, j, 0)
@@ -348,7 +350,7 @@
         def _(i):
             part = pl.ds(pl.multiple_of(i * 256, 256), 256)
             tile = dot(
-                home[3, j].reshape(FR, CH), w[0, j, :, :, part].reshape(CH, 256), NN
+                home[3, j].reshape(FR, CH), out_rows(j, part), NN
             )
             tile = tile + (x_ref[:, part].astype(F32) if first else total[:, part])
             if last:
@@ -379,7 +381,7 @@
     tick1(0)
     landed(0)
     tick0(5), tick2(0), tick1(5), tick3(0), tick2(5)
-    for j in range(1, NCH):
+    for j in range(1, NG):
         for m in (1, 2, 3):
             swap(m, j)
     loads[1].wait()
@@ -396,23 +398,23 @@
     projections(2)
     tick2(4), tick3(4), tick4(4)
     projections(3)
-    attend(0)
-    attend(1)
-    lift((0, 1))
-    attend(2)
-    lift((2, 3))
-    attend(3)
-    order = [j for j in range(NCH) if j != LOW] + [LOW]
-    for j in order:
+    @pl.loop(0, NCH)
+    def _(j):
+        attend(j)
+        pl.when(j == LOW)(lambda: lift((0, 1)))
+        pl.when(j == LOW + 1)(lambda: lift((2, 3)))
+
+    for j in range(NCH):
         rest(j)
-    for j in order:
-        finish(j, j == order[0], j == order[-1])
+    for j in range(NCH):
+        finish(j, j == 0, j == NCH - 1)
 
     copies["z", 0, 0].wait_send()
-    for j in range(NCH):
+    for j in range(NG):
         for m in (1, 2, 3):
             copies["z", m, j].wait_send()
 
+    for j in range(NCH):
         @pl.when(jnp.logical_or(upper == 0, j != LOW))
         def _():
             for t in range(4):
@@ -430,7 +432,7 @@
                 for t in range(2):
                     drain(homex, bxsend, t, j)
 
-    for p in range(2 + NCH):
+    for p in range(2 + NG):
         for s in range(1, 17):
             copies[p, s].wait_send()
 
@@ -463,10 +465,10 @@
             pltpu.VMEM((4, GR, FG, CH), BF), four, two,
             pltpu.VMEM((FR, D), F32),
             pltpu.VMEM((FR, D), F32),
-            pltpu.SemaphoreType.DMA((1 + 3 * NCH,)),
-            pltpu.SemaphoreType.DMA((1 + 3 * NCH,)),
-            pltpu.SemaphoreType.DMA((2 + NCH, 17)),
-            pltpu.SemaphoreType.DMA((2 + NCH, 17)),
+            pltpu.SemaphoreType.DMA((1 + 3 * NG,)),
+            pltpu.SemaphoreType.DMA((1 + 3 * NG,)),
+            pltpu.SemaphoreType.DMA((2 + NG, 17)),
+            pltpu.SemaphoreType.DMA((2 + NG, 17)),
             pltpu.SemaphoreType.DMA((4,)),
             pltpu.SemaphoreType.DMA((2,)),
             sem4, sem4, sem2, sem2,

time: 209 us -> 209 us (level)
  the two profiles are of different devices: /device:TPU:1 before, /device:TPU:481 now
where the time goes in v4:
time: 209 us; the launch traced here: 208 us
  Pallas kernels  205 us (98%)
  local copies, waits for them, and re-layouts  2.72 us (1%)
    pallas_call x1, Pallas kernels, body(): pl.pallas_call(kernel, out_shape=[jax.ShapeDtypeStruct((FR, D), BF)] * 2,...  205 us

profile of v4, /device:TPU:481, one launch (start us, length us, event | category | flops | bytes accessed | tf_op | source)
XLA Modules:
  0.0 208.4 jit_solution(1599152234556080877)
XLA Ops:
  0.6 205.1 %shard_map.68 = (bf16[256,1024]{1,0:T(8,128)(2,1)}, bf16[256,1024]{1,0:T(8,128)(2,1)}) custom-call(bf16[256,1024]{1,0:T(8,128)(2,1)} %bitcast.7, f32[1,1024]{1,0:T(1,128)} %bitcast.13, bf16[32,3072]{1,0:T(8,128)(2,1)} %bitcast.11, bf16[32,1024]{1,0:T(8,128)(2,1)} %bitcast.12, bf16[256,1024]{1,0:T(8,128)(2,1)} %bitcast.8), custom_call_target="tpu_custom_call" | custom-call | tf_op jit(solution)/shard_map/pallas_call | solution.py:454
  205.7 0.0 copy-start
  205.7 1.9 copy.9
  207.6 0.0 copy-done
  207.6 0.8 copy.10
Async XLA Ops:
  205.7 1.9 copy-start
